TPU v7x, 256 devices: a whole 4x4x8 slice. The times are simulated.
256 devices in a mesh: fsdp: 16 (over z, x_hi), dp: 16 (over y, x_lo, core).
Axes of the slice: x: 4 (x_hi: 2, x_lo: 2; x = x_hi * 2 + x_lo), y: 4, z: 8, core: 2. Of those that a mesh axis runs over, the one named last changes fastest.
Arguments:
- features: bfloat16 [65536, 1024], P(('fsdp', 'dp')), may hold values from -24 to 24
- normed: bfloat16 [65536, 4096], P(('fsdp', 'dp')), may hold values from -6 to 6
- relu_mask: int32 [65536, 4096], P(('fsdp', 'dp')), may hold values 0 or 1
- cotangent: bfloat16 [65536, 4096], P(('fsdp', 'dp')), may hold values from -40 to 40
- weight_shard: bfloat16 [1024, 4096], P('fsdp'), may hold values from -0.1875 to 0.1875
- norm_gain: float32 [4096], replicated, may hold values from 0.25 to 1.75
- inverse_deviation: float32 [4096], replicated, may hold values from 0.5 to 3
Outputs:
- grad_input: bfloat16 [65536, 1024], P(('fsdp', 'dp'))
- grad_weight: float32 [1024, 4096], P('fsdp')
- grad_gain: float32 [4096], replicated
- grad_shift: float32 [4096], replicated
All inputs are finite; a program needn't handle non-finite values. No bound on the sum of `relu_mask` on one device may be relied on, other than what follows from the above.
Results may differ from a plain program's by a relative error of at most 0.005.
Values may be sent and summed in bfloat16 or wider, within the bound.
A program may use at most 128 MiB of HBM per device.

v0:
```python
import functools
import math

import jax
import jax.numpy as jnp
from jax import lax
from jax.sharding import Mesh
from jax.sharding import PartitionSpec as P

FSDP = ("fsdp_0", "fsdp_1")
DP = ("dp_0", "dp_1", "dp_2")
FSDP_DP = ("fsdp_0", "fsdp_1", "dp_0", "dp_1", "dp_2")


def one_axis_at_a_time(value, axes):
    return functools.reduce(lax.psum, axes, value)


def in_blocks(value, dim, peers):
    lengths = value.shape
    tiles = value.reshape(*lengths[:dim], peers, lengths[dim] // peers, *lengths[dim + 1 :])
    return jnp.moveaxis(tiles, dim, 0)


def summed_on_arrival(value, axis, dim):
    tiles = in_blocks(value, dim, lax.axis_size(axis))
    arrived = lax.all_to_all(tiles, axis, split_axis=0, concat_axis=0, tiled=True)
    return arrived.sum(axis=0)


def copy_for_each(value, axis):
    copies = jnp.broadcast_to(value, (lax.axis_size(axis), *value.shape))
    return lax.all_to_all(copies, axis, split_axis=0, concat_axis=0, tiled=True)


def in_order(tiles, dim):
    tiles = jnp.moveaxis(tiles, 0, dim)
    lengths = tiles.shape
    return tiles.reshape(*lengths[:dim], lengths[dim] * lengths[dim + 1], *lengths[dim + 2 :])


def gather_directly(value, axis, dim):
    tiles = copy_for_each(value, axis)
    return in_order(tiles, dim)


def on_device(features, normed, relu_mask, cotangent, weight_shard, norm_gain, inverse_deviation):
    local_rows = features.shape[0]
    total_rows = local_rows * lax.axis_size(FSDP) * lax.axis_size(DP)
    masked = cotangent.astype(jnp.float32) * relu_mask.astype(jnp.float32)
    normed_f = normed.astype(jnp.float32)
    local_plain = jnp.sum(masked, axis=0)
    local_cross = jnp.sum(masked * normed_f, axis=0)
    sum_plain, sum_cross = (
        one_axis_at_a_time(local_plain, FSDP_DP),
        one_axis_at_a_time(local_cross, FSDP_DP),
    )
    norm_grad = (
        inverse_deviation
        * norm_gain
        * (masked - sum_plain / total_rows - normed_f * (sum_cross / total_rows))
    )
    norm_grad = norm_grad.astype(jnp.bfloat16)
    grad_input = lax.dot_general(
        norm_grad,
        lax.all_gather(weight_shard, FSDP, axis=0, tiled=True),
        (((1,), (1,)), ((), ())),
        preferred_element_type=jnp.float32,
    ).astype(jnp.bfloat16)
    unit_block = lax.all_to_all(norm_grad, DP, split_axis=1, concat_axis=0, tiled=True)
    unit_term = lax.dot_general(
        lax.all_gather(features, DP, axis=0, tiled=True),
        unit_block,
        (((0,), (0,)), ((), ())),
        preferred_element_type=jnp.float32,
    )
    owner_part = summed_on_arrival(unit_term, FSDP, 0)
    summed = gather_directly(owner_part, DP, 1)
    rescale = 1.0 / math.sqrt(total_rows)
    return (grad_input, summed * rescale, sum_cross * rescale, sum_plain * rescale)


def solution(mesh):
    split = Mesh(mesh.devices.reshape(8, 2, 4, 2, 2), ("fsdp_0", "fsdp_1", "dp_0", "dp_1", "dp_2"))
    return jax.shard_map(
        on_device,
        mesh=split,
        in_specs=(
            P(FSDP_DP, None),
            P(FSDP_DP, None),
            P(FSDP_DP, None),
            P(FSDP_DP, None),
            P(FSDP, None),
            P(),
            P(),
        ),
        out_specs=(P(FSDP_DP, None), P(FSDP, None), P(), P()),
        check_vma=False,
    )
```

profile of v0, /device:TPU:1, one launch (start us, length us, event | category | flops | bytes accessed | tf_op | source)
XLA Modules:
  0.0 235.0 jit_solution(161861587621156567)
XLA Ops:
  7.2 0.0 all-gather.5.cloned.1.call-start
  7.2 0.7 all-gather.5.cloned.1.call-update
  7.9 0.0 all-gather.3.cloned.1.call-start
  7.9 0.7 all-gather.3.cloned.1.call-update
  8.6 3.3 %copy.24 = bf16[256,4096]{0,1:T(8,128)(2,1)S(1)} copy(bf16[256,4096]{1,0:T(8,128)(2,1)} %param.8) | data formatting | bytes 4194304 | tf_op args[1]
  11.9 5.6 %copy.23 = s32[256,4096]{0,1:T(8,128)} copy(s32[256,4096]{1,0:T(8,128)} %param.9) | data formatting | bytes 8388608 | tf_op args[2]
  17.5 0.0 copy-start.2
  17.5 0.0 copy-start.3
  17.5 4.1 %copy.22 = bf16[256,4096]{0,1:T(8,128)(2,1)} copy(bf16[256,4096]{1,0:T(8,128)(2,1)} %param.10) | data formatting | bytes 4194304 | tf_op args[3]
  21.7 0.0 copy-done.2
  21.7 0.0 copy-done.3
  21.7 4.1 %fusion.4 = (f32[4096]{0:T(1024)S(1)}, f32[4096]{0:T(1024)S(1)}) fusion(s32[256,4096]{0,1:T(8,128)} %copy.23, bf16[256,4096]{0,1:T(8,128)(2,1)} %copy.22, bf16[256,4096]{0,1:T(8,128)(2,1)S(1)} %copy.24), kind=kLoop, calls=%fused_computation.7 | loop fusion | flops 7331840 | bytes 8421376 | tf_op jit(solution)/shard_map/reduce_sum | solution.py:52
  25.7 26.9 %all-reduce = (f32[4096]{0:T(1024)S(1)}, f32[4096]{0:T(1024)S(1)}) all-reduce(f32[4096]{0:T(1024)S(1)} %get-tuple-element.5, f32[4096]{0:T(1024)S(1)} %get-tuple-element.4), channel_id=1, replica_groups=mesh['fsdp_0'=8,'fsdp_1'=2,'dp_0'=4,'dp_1'=2,'dp_2'=2] {'fsdp_0'}, use_global_device_ids=true, to_apply=%region_7.0 | all-reduce | flops 8192 | bytes 65536 | tf_op jit(solution)/shard_map/psum | solution.py:16
  52.6 10.4 %all-reduce.4 = (f32[4096]{0:T(1024)S(1)}, f32[4096]{0:T(1024)S(1)}) all-reduce(f32[4096]{0:T(1024)S(1)} %get-tuple-element.6, f32[4096]{0:T(1024)S(1)} %get-tuple-element.7), channel_id=1, replica_groups=mesh['fsdp_0'=8,'fsdp_1'=2,'dp_0'=4,'dp_1'=2,'dp_2'=2] {'fsdp_1'}, use_global_device_ids=true, to_apply=%region_8.0 | all-reduce | flops 8192 | bytes 65536 | tf_op jit(solution)/shard_map/psum | solution.py:16
  63.0 13.4 %all-reduce.1 = (f32[4096]{0:T(1024)S(1)}, f32[4096]{0:T(1024)S(1)}) all-reduce(f32[4096]{0:T(1024)S(1)} %get-tuple-element.14, f32[4096]{0:T(1024)S(1)} %get-tuple-element.15), channel_id=1, replica_groups=mesh['fsdp_0'=8,'fsdp_1'=2,'dp_0'=4,'dp_1'=2,'dp_2'=2] {'dp_0'}, use_global_device_ids=true, to_apply=%region_9.0 | all-reduce | flops 8192 | bytes 65536 | tf_op jit(solution)/shard_map/psum | solution.py:16
  76.3 5.6 %all-reduce.3 = (f32[4096]{0:T(1024)S(1)}, f32[4096]{0:T(1024)S(1)}) all-reduce(f32[4096]{0:T(1024)S(1)} %get-tuple-element.8, f32[4096]{0:T(1024)S(1)} %get-tuple-element.9), channel_id=1, replica_groups=mesh['fsdp_0'=8,'fsdp_1'=2,'dp_0'=4,'dp_1'=2,'dp_2'=2] {'dp_1'}, use_global_device_ids=true, to_apply=%region_10.0 | all-reduce | flops 8192 | bytes 65536 | tf_op jit(solution)/shard_map/psum | solution.py:16
  81.9 17.9 %all-reduce.2 = (f32[4096]{0:T(1024)S(1)}, f32[4096]{0:T(1024)S(1)}) all-reduce(f32[4096]{0:T(1024)S(1)} %get-tuple-element.12, f32[4096]{0:T(1024)S(1)} %get-tuple-element.13), channel_id=1, replica_groups=mesh['fsdp_0'=8,'fsdp_1'=2,'dp_0'=4,'dp_1'=2,'dp_2'=2] {'dp_2'}, use_global_device_ids=true, to_apply=%region_11.0 | all-reduce | flops 8192 | bytes 65536 | tf_op jit(solution)/shard_map/psum | solution.py:16
  99.9 0.6 broadcast_multiply_fusion
  100.5 4.3 %fusion.3 = bf16[256,4096]{0,1:T(8,128)(2,1)S(1)} fusion(bf16[256,4096]{0,1:T(8,128)(2,1)S(1)} %copy.24, f32[4096]{0:T(1024)S(1)} %get-tuple-element.20, f32[4096]{0:T(1024)S(1)} %get-tuple-element.17, f32[4096]{0:T(1024)S(1)} %mul.43, s32[256,4096]{0,1:T(8,128)} %copy.23, bf16[256,4096]{0,1:T(8,128)(2,1)} %copy.22), kind=kLoop, calls=%fused_computation.5 | loop fusion | flops 9437184 | bytes 10534912 | tf_op jit(solution)/shard_map/convert_element_type | solution.py:63
  104.9 0.0 copy-start
  104.9 35.0 %all_to_all.29 = bf16[256,16,256]{0,2,1:T(8,128)(2,1)} all-to-all(bf16[256,16,256]{0,2,1:T(8,128)(2,1)S(1)} %bitcast.15), channel_id=1, replica_groups=mesh['fsdp_0'=8,'fsdp_1'=2,'dp_0'=4,'dp_1'=2,'dp_2'=2] {'dp_0','dp_1','d..., dimensions={1} | all-to-all | bytes 4194304 | tf_op jit(solution)/shard_map/all_to_all | solution.py:70
  139.9 0.0 copy-done
  139.9 2.8 %copy.25 = bf16[16,256,256]{2,1,0:T(8,128)(2,1)S(1)} copy(bf16[16,256,256]{1,2,0:T(8,128)(2,1)} %bitcast.16) | data formatting | bytes 4194304 | tf_op jit(solution)/shard_map/all_to_all | solution.py:70
  142.7 0.0 all-gather.5.cloned.1.call-done
  142.7 5.7 %convolution_bitcast_fusion = f32[1024,256]{0,1:T(8,128)S(1)} fusion(bf16[4096,256]{1,0:T(8,128)(2,1)S(1)} %bitcast.14, bf16[4096,1024]{1,0:T(8,128)(2,1)} %all-gather.5.cloned.1.call-done), kind=kOutput, calls=%fused_computation.8 | convolution fusion | flops 2147483648 | bytes 11534336 | tf_op jit(solution)/shard_map/dot_general | solution.py:71
  148.5 0.0 copy-start.1
  148.5 1.3 copy.26
  149.8 35.3 %all_to_all.30 = f32[16,64,256]{2,1,0:T(8,128)S(1)} all-to-all(f32[16,64,256]{2,1,0:T(8,128)} %bitcast.17), channel_id=1, replica_groups=mesh['fsdp_0'=8,'fsdp_1'=2,'dp_0'=4,'dp_1'=2,'dp_2'=2] {'fsdp_0','fsdp_1'}, dimensions={0} | all-to-all | bytes 2097152 | tf_op jit(solution)/shard_map/all_to_all | solution.py:27
  185.1 0.1 reduce_sum.29
  185.1 1.1 broadcast_in_dim.2
  186.2 6.3 %all-to-all-start.2 = ((f32[16,64,256]{2,1,0:T(8,128)}), f32[16,64,256]{2,1,0:T(8,128)S(1)}, u32[]{:S(2)}, u32[]{:S(2)}) async-start(f32[16,64,256]{2,1,0:T(8,128)} %broadcast_in_dim.2), calls=%async_computation.2 | async-start | bytes 2097152 | tf_op jit(solution)/shard_map/all_to_all | solution.py:33
  192.5 28.0 %all-gather.3.cloned.1.call-done = bf16[1024,4096]{1,0:T(8,128)(2,1)} async-done(((bf16[64,4096]{1,0:T(8,128)(2,1)}), bf16[1024,4096]{1,0:T(8,128)(2,1)}) %all-gather.3.cloned.1.call-update) | async-done | bytes 8388624 | tf_op jit(solution)/shard_map/all_gather | solution.py:66
  220.4 0.0 copy-done.1
  220.4 6.6 %convolution_convert_fusion = bf16[256,1024]{1,0:T(8,128)(2,1)} fusion(bf16[256,4096]{0,1:T(8,128)(2,1)S(1)} %copy-done.1, bf16[1024,4096]{1,0:T(8,128)(2,1)} %all-gather.3.cloned.1.call-done), kind=kOutput, calls=%fused_computation.9 | convolution fusion | flops 2147745792 | bytes 11010048 | tf_op jit(solution)/shard_map/dot_general | solution.py:64
  227.0 0.0 all-to-all-done.2
  227.0 0.1 multiply_bitcast_fusion
  227.1 1.1 copy.28
  (1 shorter events, 0.0 us)
Async XLA Ops:
  7.2 135.6 %all-gather.5.cloned.1.call-start = ((), (), s32[]{:S(2)}) async-start(), calls=%async_computation.4 | async-start | bytes 8912896 | tf_op jit(solution)/shard_map/all_gather | solution.py:72
  7.9 212.5 %all-gather.3.cloned.1.call-start = ((), (), s32[]{:S(2)}) async-start(), calls=%async_computation.3 | async-start | bytes 8912896 | tf_op jit(solution)/shard_map/all_gather | solution.py:66
  17.5 4.1 %copy-start.2 = (f32[4096]{0:T(1024)S(1)}, f32[4096]{0:T(1024)}, u32[]{:S(2)}) copy-start(f32[4096]{0:T(1024)} %param.13) | copy-start | bytes 49156
  17.5 4.1 %copy-start.3 = (f32[4096]{0:T(1024)S(1)}, f32[4096]{0:T(1024)}, u32[]{:S(2)}) copy-start(f32[4096]{0:T(1024)} %param.12) | copy-start | bytes 49156
  104.9 35.0 %copy-start = (bf16[256,4096]{0,1:T(8,128)(2,1)}, bf16[256,4096]{0,1:T(8,128)(2,1)S(1)}, u32[]{:S(2)}) copy-start(bf16[256,4096]{0,1:T(8,128)(2,1)S(1)} %fusion.3) | copy-start | bytes 6291460
  148.5 72.0 %copy-start.1 = (bf16[256,4096]{0,1:T(8,128)(2,1)S(1)}, bf16[256,4096]{0,1:T(8,128)(2,1)}, u32[]{:S(2)}) copy-start(bf16[256,4096]{0,1:T(8,128)(2,1)} %copy-done) | copy-start | bytes 6291460
  186.2 40.8 %all-to-all-start.2 = ((f32[16,64,256]{2,1,0:T(8,128)}), f32[16,64,256]{2,1,0:T(8,128)S(1)}, u32[]{:S(2)}, u32[]{:S(2)}) async-start(f32[16,64,256]{2,1,0:T(8,128)} %broadcast_in_dim.2), calls=%async_computation.2 | async-start | bytes 2097152 | tf_op jit(solution)/shard_map/all_to_all | solution.py:33
Sparse Core Ops, SparseCore 0:
  9.8 59.1 all-gather.4
  71.6 148.7 all-gather.2
where the time goes:
time: 236 us; the launch traced here: 235 us
  blocking collectives  144 us (61%)
  waiting for transfers between devices  29.4 us (12%)
  local copies, waits for them, and re-layouts  19.3 us (8%)
  between operations  14.1 us (6%)
  matrix products  12.3 us (5%)
  other arithmetic  9.19 us (4%)
  starting transfers between devices  6.36 us (3%)
    psum x5, blocking collectives, one_axis_at_a_time(): return functools.reduce(lax.psum, axes, value)  74.1 us
    all_to_all x1, blocking collectives, summed_on_arrival(): lax.all_to_all(tiles, axis, split_axis=0, concat_axis=0, tiled=True)  35.3 us
    all_to_all x1, blocking collectives, on_device(): lax.all_to_all(norm_grad, DP, split_axis=1, concat_axis=0, tiled=True)  35 us
    all_gather x1, waiting for transfers between devices, on_device(): lax.all_gather(weight_shard, FSDP, axis=0, tiled=True)  28 us
    unnamed x11, local copies, waits for them, and re-layouts  13 us
    dot_general x1, matrix products, on_device(): lax.dot_general(norm_grad, lax.all_gather(weight_shard, FSDP, axis=0, til...  6.56 us
    all_to_all x1, starting transfers between devices, copy_for_each(): return lax.all_to_all(copies, axis, split_axis=0, concat_axis=0, tiled=True)  6.28 us
    dot_general x1, matrix products, on_device(): lax.dot_general(lax.all_gather(features, DP, axis=0, tiled=True), unit_bl...  5.73 us
  transfers between devices with their start and end apart: 3, of which 1 were waited for; matrix products, arithmetic and copies ran while one was open for 17% of the time, Pallas kernels for 0%

commit v1 on v0

v1 whole, which is shorter than its diff:
```python
import math

import jax
import jax.numpy as jnp
from jax import lax
from jax.experimental import pallas as pl
from jax.experimental.pallas import tpu as pltpu
from jax.sharding import Mesh
from jax.sharding import PartitionSpec as P

Z, XH, Y, XL, C = "z", "xh", "y", "xl", "c"
NZ, NX, NY = 8, 4, 4
F32, BF16 = jnp.float32, jnp.bfloat16

ROWS = 256
DIN = 1024
DOUT = 4096
LANES = 128
BLOCKS = DOUT // LANES
CHUNKS = BLOCKS // (NY * 2)
HALF = BLOCKS // 2
GROUPS = 4

STAGE_X = BF16
STAGE_Z = BF16


def body(
    feat_hbm, normed_hbm, mask_hbm, cot_hbm, w_hbm, gain_hbm, inv_hbm,
    gi_hbm, gw_hbm, stat_hbm,
    feat, normed, mask, cot, scale_a, scale_b, msk, wf, ft, ngs, ngr, rel,
    xs, xr, zs, zr, gw, gi, acc, st, st_core, st_z, st_x, st_y, st_all,
    load_sem, out_sem,
    sc_s, sc_r, sz_s, sz_r, sx_s, sx_r, sy_s, sy_r, sa_s, sa_r,
    f_s, f_r, fp_s, fp_r,
    wo_s, wo_r, wz_s, wz_r, wp_s, wp_r,
    ng_s, ng_r, rl_s, rl_r, fw_s,
    x_s, x_r, z_s, z_r, g_s, g_r, gp_s, gp_r,
):
    z, xh, y, xl, c = (lax.axis_index(name) for name in (Z, XH, Y, XL, C))
    x = 2 * xh + xl
    oc, oxh, oxl = 1 - c, 1 - xh, 1 - xl
    yp, ym, y2 = (y + 1) % NY, (y + 3) % NY, (y + 2) % NY
    zp, zm = (z + 1) % NZ, (z + NZ - 1) % NZ
    me = 2 * y + c
    partner = {C: oc}
    x_peers = [(oxh, oxl), (xh, oxl), (oxh, xl)]
    sent = []

    def send(src, dst, ss, rs, device):
        copy = pltpu.make_async_remote_copy(
            src_ref=src, dst_ref=dst, send_sem=ss, recv_sem=rs,
            device_id=device, device_id_type=pl.DeviceIdType.MESH,
        )
        copy.start()
        sent.append(copy)

    def arrived(dst, ss, rs):
        pltpu.make_async_remote_copy(
            src_ref=dst, dst_ref=dst, send_sem=ss, recv_sem=rs,
            device_id=partner, device_id_type=pl.DeviceIdType.MESH,
        ).wait_recv()

    load_feat = pltpu.make_async_copy(feat_hbm, feat, load_sem.at[0])
    load_w = pltpu.make_async_copy(w_hbm, wf.at[z, xh], load_sem.at[1])
    load_a = pltpu.make_async_copy(gain_hbm, scale_a, load_sem.at[2])
    load_b = pltpu.make_async_copy(inv_hbm, scale_b, load_sem.at[3])
    loads = []
    width = DOUT // GROUPS
    load_feat.start()
    for group in range(GROUPS):
        cols = pl.ds(group * width, width)
        loads.append([
            pltpu.make_async_copy(src.at[:, cols], dst.at[:, cols], load_sem.at[4 + 3 * group + k])
            for k, (src, dst) in enumerate(((cot_hbm, cot), (mask_hbm, mask), (normed_hbm, normed)))
        ])
        for copy in loads[-1]:
            copy.start()
    load_w.start()
    load_a.start()
    load_b.start()

    barrier = pltpu.get_barrier_semaphore()
    friends = [partner]
    for other in (yp, ym, y2):
        friends += [{Y: other, C: c}, {Y: other, C: oc}, {Y: other, XL: oxl}]
    friends += [{XH: a, XL: b} for a, b in x_peers]
    friends += [{Z: (z + k) % NZ} for k in range(1, NZ)]
    for friend in friends:
        pl.semaphore_signal(barrier, inc=1, device_id=friend, device_id_type=pl.DeviceIdType.MESH)

    load_feat.wait()
    for k in range(DIN // LANES):
        part = feat[:, k * LANES:(k + 1) * LANES]
        ft[me, k * LANES:(k + 1) * LANES, :] = part.T

    pl.semaphore_wait(barrier, len(friends))

    send(ft.at[me], ft.at[me], f_s.at[0], f_r.at[0], {Y: yp})
    send(ft.at[me], ft.at[me], f_s.at[1], f_r.at[1], {Y: ym})
    load_w.wait()
    outer = {XH: oxh, XL: oxl}
    send(wf.at[z, xh, c], wf.at[z, xh, c], wo_s.at[0], wo_r.at[0], outer)

    per_group = BLOCKS // GROUPS
    for group in range(GROUPS):
        for copy in loads[group]:
            copy.wait()

        def sums(i, carry):
            b = group * per_group + i
            cols = pl.ds(pl.multiple_of(b * LANES, LANES), LANES)
            value = jnp.where(mask[:, cols] != 0, cot[:, cols].astype(F32), 0.0)
            msk[b] = value.astype(BF16)
            half, row = b // HALF, b % HALF
            st[half, pl.ds(row, 1), :] = jnp.sum(value, axis=0, keepdims=True)
            cross = value * normed[:, cols].astype(F32)
            st[half, pl.ds(HALF + row, 1), :] = jnp.sum(cross, axis=0, keepdims=True)
            return carry

        lax.fori_loop(0, per_group, sums, 0)

    send(st.at[oc], st_core.at[c], sc_s.at[0], sc_r.at[0], partner)
    arrived(st_core.at[oc], sc_s.at[0], sc_r.at[0])
    st_core[c] = st[c]
    st_z[z] = st_core[0] + st_core[1]
    for k in range(1, NZ):
        send(st_z.at[z], st_z.at[z], sz_s.at[k], sz_r.at[z], {Z: (z + k) % NZ})

    def other(o):
        return xh if o == 0 else oxh

    def weights_on(direction, step, o):
        block = (z - (step - 1)) % NZ if direction == 0 else (z + (step - 1)) % NZ
        ref = wf.at[block, other(o), c]
        send(ref, ref, wz_s.at[direction, step - 1, o], wz_r.at[direction, step - 1, o],
             {Z: zp if direction == 0 else zm})

    def weights_in(direction, step, o):
        block = (z - step + NZ) % NZ if direction == 0 else (z + step) % NZ
        ref = wf.at[block, other(o), c]
        arrived(ref, wz_s.at[direction, step - 1, o], wz_r.at[direction, step - 1, o])
        send(ref, ref, wp_s.at[direction, step - 1, o], wp_r.at[direction, step - 1, o], partner)

    def weights_over(direction, step, o):
        block = (z - step + NZ) % NZ if direction == 0 else (z + step) % NZ
        ref = wf.at[block, other(o), oc]
        arrived(ref, wp_s.at[direction, step - 1, o], wp_r.at[direction, step - 1, o])

    def weights_next(step, o):
        for direction in range(2):
            if step == 4:
                if direction == o:
                    weights_in(direction, step, o)
                continue
            block_in = (z - step + NZ) % NZ if direction == 0 else (z + step) % NZ
            ref = wf.at[block_in, other(o), c]
            arrived(ref, wz_s.at[direction, step - 1, o], wz_r.at[direction, step - 1, o])
            if step < 3 or direction == o:
                send(ref, ref, wz_s.at[direction, step, o], wz_r.at[direction, step, o],
                     {Z: zp if direction == 0 else zm})
            send(ref, ref, wp_s.at[direction, step - 1, o], wp_r.at[direction, step - 1, o], partner)

    weights_on(0, 1, 0)
    weights_on(1, 1, 0)
    arrived(wf.at[z, oxh, c], wo_s.at[0], wo_r.at[0])
    weights_on(0, 1, 1)
    weights_on(1, 1, 1)
    send(wf.at[z, oxh, c], wf.at[z, oxh, c], wp_s.at[0, 3, 1], wp_r.at[0, 3, 1], partner)

    for k in range(1, NZ):
        source = (z + k) % NZ
        arrived(st_z.at[source], sz_s.at[k], sz_r.at[source])
    st_x[x] = sum((st_z[k] for k in range(1, NZ)), st_z[0])
    for k, (a, b) in enumerate(x_peers):
        send(st_x.at[x], st_x.at[x], sx_s.at[k], sx_r.at[x], {XH: a, XL: b})
    for k, (a, b) in enumerate(x_peers):
        source = 2 * a + b
        arrived(st_x.at[source], sx_s.at[k], sx_r.at[source])
    st_y[y] = st_x[0] + st_x[1] + st_x[2] + st_x[3]
    for k in range(1, NY):
        send(st_y.at[y], st_y.at[y], sy_s.at[k], sy_r.at[y], {Y: (y + k) % NY})

    mid = DIN // 2
    send(ft.at[me], ft.at[me], fp_s.at[0], fp_r.at[0], partner)
    low, high = ft.at[2 * ym + c], ft.at[2 * yp + c]
    arrived(low, f_s.at[0], f_r.at[0])
    part = ft.at[2 * ym + c, pl.ds(0, mid)]
    send(part, part, f_s.at[2], f_r.at[2], {Y: yp})
    arrived(high, f_s.at[1], f_r.at[1])
    part = ft.at[2 * yp + c, pl.ds(mid, mid)]
    send(part, part, f_s.at[3], f_r.at[3], {Y: ym})
    send(low, low, fp_s.at[1], fp_r.at[1], partner)
    send(high, high, fp_s.at[2], fp_r.at[2], partner)

    for k in range(1, NY):
        source = (y + k) % NY
        arrived(st_y.at[source], sy_s.at[k], sy_r.at[source])
    st_all[c] = st_y[0] + st_y[1] + st_y[2] + st_y[3]
    send(st_all.at[c], st_all.at[c], sa_s.at[0], sa_r.at[0], partner)
    load_a.wait()
    load_b.wait()
    arrived(st_all.at[oc], sa_s.at[0], sa_r.at[0])
    store_stat = pltpu.make_async_copy(st_all, stat_hbm, out_sem.at[0])
    store_stat.start()

    inverse_rows = 1.0 / (ROWS * NZ * NX * NY * 2)

    def norm_grad(j):
        def one(i, carry):
            b = i * CHUNKS + j
            cols = pl.ds(pl.multiple_of(b * LANES, LANES), LANES)
            half, row = b // HALF, b % HALF
            plain = st_all[half, pl.ds(row, 1), :] * inverse_rows
            cross = st_all[half, pl.ds(HALF + row, 1), :] * inverse_rows
            scale = scale_b[pl.ds(b, 1), :] * scale_a[pl.ds(b, 1), :]
            value = msk[b].astype(F32) - plain - normed[:, cols].astype(F32) * cross
            ngs[b] = (scale * value).astype(BF16)
            return carry

        lax.fori_loop(0, NY * 2, one, 0)
        ngr[j, me] = ngs[me * CHUNKS + j]

    def block(chip, core, j):
        return ngs.at[(chip * 2 + core) * CHUNKS + j]

    def send_far(j):
        send(block(y2, 0, j), rel.at[0, j], rl_s.at[0, j], rl_r.at[0, j], {Y: yp})
        send(block(y2, 1, j), rel.at[1, j], rl_s.at[1, j], rl_r.at[1, j], {Y: ym})

    def send_near(j):
        for k, chip in enumerate((yp, ym)):
            for core in range(2):
                send(block(chip, core, j), ngr.at[j, me], ng_s.at[j, 2 * k + core], ng_r.at[j, me],
                     {Y: chip, C: core})
        send(block(y, oc, j), ngr.at[j, me], ng_s.at[j, 4], ng_r.at[j, me], partner)

    def pass_on(j):
        arrived(rel.at[0, j], rl_s.at[0, j], rl_r.at[0, j])
        source = 2 * ym + c
        send(rel.at[0, j], ngr.at[j, source], fw_s.at[0, j], ng_r.at[j, source], {Y: yp, C: 0})
        arrived(rel.at[1, j], rl_s.at[1, j], rl_r.at[1, j])
        source = 2 * yp + c
        send(rel.at[1, j], ngr.at[j, source], fw_s.at[1, j], ng_r.at[j, source], {Y: ym, C: 1})

    def multiply(j):
        for k in range(1, NY * 2):
            source = (me + k) % (NY * 2)
            arrived(ngr.at[j, source], ng_s.at[j, 0], ng_r.at[j, source])
        tall = 256

        def tile(i, carry):
            rows = pl.ds(pl.multiple_of(i * tall, tall), tall)
            left = jnp.concatenate([ft[s, rows, :] for s in range(NY * 2)], axis=1)
            right = jnp.concatenate([ngr[j, s] for s in range(NY * 2)], axis=0)
            out = jnp.dot(left, right, preferred_element_type=F32).astype(STAGE_X)
            each = DIN // NZ
            share = each // NX
            for a in range(tall // each):
                for b in range(NX):
                    xs[j, b, i * (tall // each) + a] = out[a * each + b * share:a * each + (b + 1) * share]
            return carry

        lax.fori_loop(0, DIN // tall, tile, 0)
        for k, (a, b) in enumerate(x_peers):
            send(xs.at[j, 2 * a + b], xr.at[j, x], x_s.at[j, k], x_r.at[j, x], {XH: a, XL: b})
        xr[j, x] = xs[j, x]

    def over_x(j):
        for k, (a, b) in enumerate(x_peers):
            source = 2 * a + b
            arrived(xr.at[j, source], x_s.at[j, k], x_r.at[j, source])
        total = xr[j, 0].astype(F32)
        for k in range(1, NX):
            total += xr[j, k].astype(F32)
        zs[j] = total.astype(STAGE_Z)
        for k in range(1, NZ):
            to = (z + k) % NZ
            send(zs.at[j, to], zr.at[j, z], z_s.at[j, k], z_r.at[j, z], {Z: to})
        zr[j, z] = zs[j, z]

    def over_z(j):
        for k in range(1, NZ):
            source = (z + k) % NZ
            arrived(zr.at[j, source], z_s.at[j, k], z_r.at[j, source])
        total = zr[j, 0].astype(F32)
        for k in range(1, NZ):
            total += zr[j, k].astype(F32)
        gw[xl, y, c, j] = total
        mine = gw.at[xl, y, c, j]
        k = 0
        for chip in (yp, ym, y2, y):
            for side in (oxl, xl):
                if chip is y and side is xl:
                    continue
                send(mine, mine, g_s.at[j, k], g_r.at[j, xl * NY + y], {Y: chip, XL: side})
                k += 1

    def gathered(j):
        for chip in (yp, ym, y2, y):
            for side in (oxl, xl):
                if chip is y and side is xl:
                    continue
                arrived(gw.at[side, chip, c, j], g_s.at[j, 0], g_r.at[j, side * NY + chip])
        part = gw.at[:, :, c, j]
        send(part, part, gp_s.at[j], gp_r.at[j], partner)

    def grad_input(p):
        acc[...] = jnp.zeros_like(acc)
        deep = 1024

        def step(i, carry):
            cols = pl.ds(pl.multiple_of(i * deep, deep), deep)
            count = deep // LANES
            left = jnp.concatenate([ngs[i * count + k] for k in range(count)], axis=1)
            right = wf[2 * p:2 * p + 2, :, :, :, cols].reshape(256, deep)
            acc[...] += lax.dot_general(left, right, (((1,), (1,)), ((), ())), preferred_element_type=F32)
            return carry

        lax.fori_loop(0, DOUT // deep, step, 0)
        gi[:, p * 256:(p + 1) * 256] = acc[...].astype(BF16)

    norm_grad(0)
    send_far(0)
    send_near(0)
    norm_grad(1)
    send_far(1)
    weights_next(1, 0)
    for j in range(CHUNKS):
        pass_on(j)
        if j + 1 < CHUNKS:
            send_near(j + 1)
        if j + 2 < CHUNKS:
            norm_grad(j + 2)
            send_far(j + 2)
        if j == 0:
            weights_next(1, 1)
            far = ft.at[2 * y2 + c]
            arrived(ft.at[2 * y2 + c, pl.ds(0, mid)], f_s.at[2], f_r.at[2])
            arrived(ft.at[2 * y2 + c, pl.ds(mid, mid)], f_s.at[3], f_r.at[3])
            send(far, far, fp_s.at[3], fp_r.at[3], partner)
            for k, chip in enumerate((y, ym, yp, y2)):
                arrived(ft.at[2 * chip + oc], fp_s.at[k], fp_r.at[k])
        multiply(j)
        if j >= 1:
            over_x(j - 1)
        if j >= 2:
            over_z(j - 2)
        if j >= 3:
            gathered(j - 3)
        if j == 0:
            weights_next(2, 0)
        if j == 1:
            weights_next(2, 1)
        if j == 2:
            weights_next(3, 0)
    weights_next(3, 1)
    over_x(3)
    over_z(2)
    gathered(1)
    weights_next(4, 0)
    weights_next(4, 1)
    arrived(wf.at[z, oxh, oc], wp_s.at[0, 3, 1], wp_r.at[0, 3, 1])
    for step in range(1, 5):
        for o in range(2):
            for direction in range(2):
                if step < 4 or direction == o:
                    weights_over(direction, step, o)
    grad_input(0)
    grad_input(1)
    over_z(3)
    gathered(2)
    grad_input(2)
    grad_input(3)
    store_gi = pltpu.make_async_copy(gi, gi_hbm, out_sem.at[1])
    store_gi.start()
    gathered(3)
    for j in range(CHUNKS):
        arrived(gw.at[:, :, oc, j], gp_s.at[j], gp_r.at[j])
    store_gw = pltpu.make_async_copy(gw, gw_hbm, out_sem.at[2])
    store_gw.start()
    for copy in sent:
        copy.wait_send()
    store_stat.wait()
    store_gi.wait()
    store_gw.wait()


def on_device(features, normed, relu_mask, cotangent, weight_shard, norm_gain, inverse_deviation):
    dma = pltpu.SemaphoreType.DMA
    vmem = pltpu.VMEM
    any_space = pl.BlockSpec(memory_space=pl.ANY)
    rows_out = DIN // (NZ * NX)
    scratch = [
        vmem((ROWS, DIN), BF16), vmem((ROWS, DOUT), BF16), vmem((ROWS, DOUT), jnp.int32), vmem((ROWS, DOUT), BF16),
        vmem((BLOCKS, LANES), F32), vmem((BLOCKS, LANES), F32), vmem((BLOCKS, ROWS, LANES), BF16),
        vmem((NZ, 2, 2, 32, DOUT), BF16), vmem((NY * 2, DIN, ROWS), BF16),
        vmem((BLOCKS, ROWS, LANES), BF16), vmem((CHUNKS, NY * 2, ROWS, LANES), BF16), vmem((2, CHUNKS, ROWS, LANES), BF16),
        vmem((CHUNKS, NX, NZ, rows_out, LANES), STAGE_X), vmem((CHUNKS, NX, NZ, rows_out, LANES), STAGE_X),
        vmem((CHUNKS, NZ, rows_out, LANES), STAGE_Z), vmem((CHUNKS, NZ, rows_out, LANES), STAGE_Z),
        vmem((2, NY, 2, CHUNKS, rows_out, LANES), F32), vmem((ROWS, DIN), BF16), vmem((ROWS, 256), F32),
        vmem((2, BLOCKS, LANES), F32), vmem((2, BLOCKS, LANES), F32), vmem((NZ, BLOCKS, LANES), F32),
        vmem((NX, BLOCKS, LANES), F32), vmem((NY, BLOCKS, LANES), F32), vmem((2, BLOCKS, LANES), F32),
        dma((4 + 3 * GROUPS,)), dma((3,)),
        dma((1,)), dma((1,)), dma((NZ,)), dma((NZ,)), dma((3,)), dma((NX,)), dma((NY,)), dma((NY,)), dma((1,)), dma((1,)),
        dma((4,)), dma((4,)), dma((4,)), dma((4,)),
        dma((1,)), dma((1,)), dma((2, 4, 2)), dma((2, 4, 2)), dma((2, 4, 2)), dma((2, 4, 2)),
        dma((CHUNKS, 5)), dma((CHUNKS, NY * 2)), dma((2, CHUNKS)), dma((2, CHUNKS)), dma((2, CHUNKS)),
        dma((CHUNKS, 3)), dma((CHUNKS, NX)), dma((CHUNKS, NZ)), dma((CHUNKS, NZ)),
        dma((CHUNKS, 7)), dma((CHUNKS, 2 * NY)), dma((CHUNKS,)), dma((CHUNKS,)),
    ]
    grad_input, pieces, sums = pl.pallas_call(
        body,
        out_shape=(
            jax.ShapeDtypeStruct((ROWS, DIN), BF16),
            jax.ShapeDtypeStruct((2, NY, 2, CHUNKS, rows_out, LANES), F32),
            jax.ShapeDtypeStruct((2, BLOCKS, LANES), F32),
        ),
        in_specs=[any_space] * 7,
        out_specs=(any_space,) * 3,
        scratch_shapes=scratch,
        compiler_params=pltpu.CompilerParams(
            collective_id=0, has_side_effects=True, vmem_limit_bytes=56 * 1024 * 1024,
        ),
    )(
        features, normed, relu_mask, cotangent, weight_shard.reshape(2, 32, DOUT),
        norm_gain.reshape(BLOCKS, LANES), inverse_deviation.reshape(BLOCKS, LANES),
    )
    rescale = 1.0 / math.sqrt(ROWS * NZ * NX * NY * 2)
    grad_weight = pieces.reshape(2, BLOCKS, rows_out, LANES).transpose(0, 2, 1, 3).reshape(2 * rows_out, DOUT) * rescale
    sums = sums.reshape(2, 2, DOUT // 2) * rescale
    return grad_input, grad_weight, sums[:, 1].reshape(DOUT), sums[:, 0].reshape(DOUT)


def solution(mesh):
    split = Mesh(mesh.devices.reshape(NZ, 2, NY, 2, 2), (Z, XH, Y, XL, C))
    rows = P((Z, XH, Y, XL, C), None)
    shard = P((Z, XH), None)
    return jax.shard_map(
        on_device,
        mesh=split,
        in_specs=(rows, rows, rows, rows, shard, P(), P()),
        out_specs=(rows, shard, P(), P()),
        check_vma=False,
    )
```

time: 236 us -> 88.4 us (0.37)
  blocking collectives: 144 us -> 0 us
  Pallas kernels: 0 us -> 81.9 us
  waiting for transfers between devices: 29.4 us -> 0 us
  local copies, waits for them, and re-layouts: 19.3 us -> 3.64 us
  between operations: 14.1 us -> 0.67 us
  matrix products: 12.3 us -> 0 us
  other arithmetic: 9.19 us -> 2.09 us
  starting transfers between devices: 6.36 us -> 0 us
    pallas_call x0 -> x1, Pallas kernels: none -> 81.9 us  [on_device(): pl.pallas_call(body, out_shape=(jax.ShapeDtypeStruct((ROWS, DIN), BF16),...]
    psum x5 -> x0, blocking collectives: 74.1 us -> none  [one_axis_at_a_time(): return functools.reduce(lax.psum, axes, value)]
    all_to_all x2 -> x0, blocking collectives: 70.3 us -> none  [the longest x1 35.3 us: summed_on_arrival(): lax.all_to_all(tiles, axis, split_axis=0, concat_axis=0, tiled=True)]
    all_gather x2 -> x0, waiting for transfers between devices: 28 us -> none  [the longest x1 28 us: on_device(): lax.all_gather(weight_shard, FSDP, axis=0, tiled=True)]
    dot_general x2 -> x0, matrix products: 12.3 us -> none  [the longest x1 6.56 us: on_device(): lax.dot_general(norm_grad, lax.all_gather(weight_shard, FSDP, axis=0, til...]
    unnamed x11 -> x4, local copies, waits for them, and re-layouts: 13 us -> 2.37 us
    all_to_all x1 -> x0, starting transfers between devices: 6.28 us -> none  [copy_for_each(): return lax.all_to_all(copies, axis, split_axis=0, concat_axis=0, tiled=True)]
    convert_element_type x1 -> x0, other arithmetic: 4.35 us -> none  [on_device(): norm_grad = norm_grad.astype(jnp.bfloat16)]
  transfers between devices with their start and end apart: 3 -> 0, of which waited for: 1 -> 0; matrix products, arithmetic and copies ran while one was open for 17% -> 0% of each run, Pallas kernels for 0% -> 0%
where the time goes in v1:
time: 88.4 us; the launch traced here: 88.3 us
  Pallas kernels  81.9 us (93%)
  local copies, waits for them, and re-layouts  3.64 us (4%)
  other arithmetic  2.09 us (2%)
    pallas_call x1, Pallas kernels, on_device(): pl.pallas_call(body, out_shape=(jax.ShapeDtypeStruct((ROWS, DIN), BF16),...  81.9 us
    unnamed x4, local copies, waits for them, and re-layouts  2.37 us

profile of v1, /device:TPU:1, one launch (start us, length us, event | category | flops | bytes accessed | tf_op | source)
XLA Modules:
  0.0 88.3 jit_solution(10312955727715121338)
XLA Ops:
  0.6 81.9 %shard_map.102 = (bf16[256,1024]{1,0:T(8,128)(2,1)}, f32[2,4,2,4,32,128]{5,4,3,2,1,0:T(8,128)}, f32[2,32,128]{2,1,0:T(8,128)}) custom-call(bf16[256,1024]{1,0:T(8,128)(2,1)} %feat_hbm.1, bf16[256,4096]{1,0:T(8,128)(2,1)} %normed_hbm.1, s32[256,4096]{1,0:T(8,128)} %mask_hbm.1, bf16[256,4096]{1,0:T(8,128)(2,1)} %cot_hbm.1, bf16[2,32,4096]{2,1,0:T(8,128)(2,1)} %bitcast.16, ...), custom_call_target="tpu_custom_call" | custom-call | tf_op jit(solution)/shard_map/pallas_call | solution.py:412
  82.5 0.8 broadcast_multiply_fusion.1
  83.3 0.6 fusion
  83.9 1.3 %broadcast_multiply_fusion = f32[2,4,2,4,32,128]{5,4,3,2,1,0:T(8,128)S(1)} fusion(f32[2,4,2,4,32,128]{5,4,3,2,1,0:T(8,128)} %get-tuple-element.8), kind=kLoop, calls=%fused_computation.1 | loop fusion | flops 262144 | bytes 2097152 | tf_op jit(solution)/shard_map/mul | solution.py:430
  85.3 0.0 copy-start
  85.3 0.6 copy.11
  85.9 1.6 %copy.14 = f32[8,8,32,128]{3,1,2,0:T(8,128)} copy(f32[8,8,32,128]{3,2,1,0:T(8,128)S(1)} %bitcast.14) | data formatting | bytes 2097152
  87.5 0.0 copy-done
  87.5 0.8 copy.16
  (1 shorter events, 0.0 us)
Async XLA Ops:
  85.3 2.2 %copy-start = (bf16[256,1024]{1,0:T(8,128)(2,1)S(1)}, bf16[256,1024]{1,0:T(8,128)(2,1)}, u32[]{:S(2)}) copy-start(bf16[256,1024]{1,0:T(8,128)(2,1)} %get-tuple-element.16) | copy-start | bytes 1572868

commit v2 on v1

v2 whole, which is shorter than its diff:
```python
import functools
import math

import jax
import jax.numpy as jnp
from jax import lax
from jax.experimental import pallas as pl
from jax.experimental.pallas import tpu as pltpu
from jax.sharding import Mesh
from jax.sharding import PartitionSpec as P

Z, XH, Y, XL, C = "z", "xh", "y", "xl", "c"
NZ, NX, NY = 8, 4, 4
F32, BF16 = jnp.float32, jnp.bfloat16

ROWS = 256
DIN = 1024
DOUT = 4096
LANES = 128
BLOCKS = DOUT // LANES
CHUNKS = BLOCKS // (NY * 2)
HALF = BLOCKS // 2
GROUPS = 4

STAGE_X = BF16
STAGE_Z = BF16


def body(
    feat_hbm, normed_hbm, mask_hbm, cot_hbm, w_hbm, gain_hbm, inv_hbm,
    gi_hbm, gw_hbm, stat_hbm,
    feat, normed, mask, cot, scale_a, scale_b, msk, wf, ft, ngs, ngr, rel,
    xs, xr, zs, zr, gw, gi, acc, near, st, st_core, st_x, st_y, st_z, st_all,
    load_sem, out_sem, stat_s, stat_r,
    f_s, f_r, fp_s, fp_r,
    wo_s, wo_r, wz_s, wz_r, wl_r, wp_s, wp_r,
    ng_s, near_r, far_r, rel_r,
    x_s, x_r, z_s, z_r, g_s, g_r, gp_s, gp_r,
):
    z, xh, y, xl, c = (lax.axis_index(name) for name in (Z, XH, Y, XL, C))
    x = 2 * xh + xl
    oc, oxh, oxl = 1 - c, 1 - xh, 1 - xl
    yp, ym, y2 = (y + 1) % NY, (y + 3) % NY, (y + 2) % NY
    zp, zm = (z + 1) % NZ, (z + NZ - 1) % NZ
    me = 2 * y + c
    partner = {C: oc}
    x_peers = [(oxh, xl), (oxh, oxl), (xh, oxl)]

    def remote(src, dst, ss, rs, device):
        return pltpu.make_async_remote_copy(
            src_ref=src, dst_ref=dst, send_sem=ss, recv_sem=rs,
            device_id=device, device_id_type=pl.DeviceIdType.MESH,
        )

    def send(src, dst, ss, rs, device):
        remote(src, dst, ss, rs, device).start()

    def arrived(ref, rs):
        remote(ref, ref, rs, rs, partner).wait_recv()

    def left(ref, ss):
        remote(ref, ref, ss, ss, partner).wait_send()

    load_feat = pltpu.make_async_copy(feat_hbm, feat, load_sem.at[0])
    load_w = pltpu.make_async_copy(w_hbm, wf.at[z, xh], load_sem.at[1])
    load_a = pltpu.make_async_copy(gain_hbm, scale_a, load_sem.at[2])
    load_b = pltpu.make_async_copy(inv_hbm, scale_b, load_sem.at[3])
    loads = []
    width = DOUT // GROUPS
    load_feat.start()
    load_w.start()
    for group in range(GROUPS):
        cols = pl.ds(group * width, width)
        loads.append([
            pltpu.make_async_copy(src.at[:, cols], dst.at[:, cols], load_sem.at[4 + 3 * group + k])
            for k, (src, dst) in enumerate(((cot_hbm, cot), (mask_hbm, mask), (normed_hbm, normed)))
        ])
        for copy in loads[-1]:
            copy.start()
    load_a.start()
    load_b.start()

    barrier = pltpu.get_barrier_semaphore()
    friends = [partner]
    for other in (yp, ym, y2):
        friends += [{Y: other, C: c}, {Y: other, C: oc}, {Y: other, XL: oxl}]
    friends += [{XH: a, XL: b} for a, b in x_peers]
    friends += [{Z: (z + k) % NZ} for k in range(1, NZ)]
    for friend in friends:
        pl.semaphore_signal(barrier, inc=1, device_id=friend, device_id_type=pl.DeviceIdType.MESH)

    load_feat.wait()
    for k in range(DIN // LANES):
        part = feat[:, k * LANES:(k + 1) * LANES]
        ft[me, k * LANES:(k + 1) * LANES, :] = part.T

    pl.semaphore_wait(barrier, len(friends))

    quarter = DIN // 4

    def feature(direction, q, late):
        ref = ft.at[me, pl.ds(q * quarter, quarter)]
        send(ref, ref, f_s.at[direction], f_r.at[late, direction], {Y: yp if direction == 0 else ym})

    feature(0, 0, 0)
    feature(1, 2, 0)
    def side(o):
        return xh if o == 0 else oxh

    def weights_on(direction, block, step, o):
        ref = wf.at[block, side(o), c]
        send(ref, ref, wz_s.at[0], wz_r.at[direction, step - 1, o], {Z: zp if direction == 0 else zm})

    def weights_next(step, o):
        blocks = [(z + NZ - step) % NZ, (z + step) % NZ]
        for direction, b in enumerate(blocks):
            arrived(wf.at[b, side(o), c], wz_r.at[direction, step - 1, o])
            if step < 3:
                weights_on(direction, b, step + 1, o)
        if step == 3:
            ref = wf.at[(z + 5 - 2 * c) % NZ, side(o), c]
            send(ref, ref, wz_s.at[0], wl_r.at[o], {Z: (z + 1 + 6 * c) % NZ})
        for b in blocks:
            ref = wf.at[b, side(o), c]
            send(ref, ref, wp_s.at[0], wp_r.at[step - 1], partner)

    def weights_last(o):
        ref = wf.at[(z + 4) % NZ, side(o), c]
        arrived(ref, wl_r.at[o])
        send(ref, ref, wp_s.at[0], wp_r.at[3], partner)

    load_w.wait()
    weights_on(0, z, 1, 0)
    weights_on(1, z, 1, 0)

    per_group = BLOCKS // GROUPS
    for group in range(GROUPS):
        for copy in loads[group]:
            copy.wait()

        def sums(i, carry):
            b = group * per_group + i
            cols = pl.ds(pl.multiple_of(b * LANES, LANES), LANES)
            value = jnp.where(mask[:, cols] != 0, cot[:, cols].astype(F32), 0.0)
            msk[b] = value.astype(BF16)
            half, row = b // HALF, b % HALF
            st[half, pl.ds(row, 1), :] = jnp.sum(value, axis=0, keepdims=True)
            cross = value * normed[:, cols].astype(F32)
            st[half, pl.ds(HALF + row, 1), :] = jnp.sum(cross, axis=0, keepdims=True)
            return carry

        lax.fori_loop(0, per_group, sums, 0)

    send(st.at[oc], st_core.at[c], stat_s.at[0], stat_r.at[0], partner)
    arrived(st_core.at[oc], stat_r.at[0])
    st_y[y] = st[c] + st_core[oc]
    for k in (2, 1, 3):
        send(st_y.at[y], st_y.at[y], stat_s.at[1], stat_r.at[1], {Y: (y + k) % NY})
    feature(0, 1, 0)
    feature(1, 3, 0)
    for late in ((2, 1), (3, 0)):
        for direction in range(2):
            feature(direction, late[direction], 1)
    arrived(st_y.at[pl.ds(0, NY - 1)], stat_r.at[1])
    st_x[x] = st_y[0] + st_y[1] + st_y[2] + st_y[3]
    for a, b in x_peers:
        send(st_x.at[x], st_x.at[x], stat_s.at[2], stat_r.at[2], {XH: a, XL: b})
    outer = {XH: oxh, XL: oxl}
    send(wf.at[z, xh, c], wf.at[z, xh, c], wo_s.at[0], wo_r.at[0], outer)
    weights_next(1, 0)
    arrived(st_x.at[pl.ds(0, NX - 1)], stat_r.at[2])
    st_z[z] = st_x[0] + st_x[1] + st_x[2] + st_x[3]
    for k in (4, 3, 5, 2, 6, 1, 7):
        send(st_z.at[z], st_z.at[z], stat_s.at[3], stat_r.at[3], {Z: (z + k) % NZ})
    mid = DIN // 2
    low, high = ft.at[2 * ym + c, pl.ds(0, mid)], ft.at[2 * yp + c, pl.ds(mid, mid)]
    arrived(low, f_r.at[0, 0])
    send(low, low, f_s.at[2], f_r.at[2, 0], {Y: yp})
    arrived(high, f_r.at[0, 1])
    send(high, high, f_s.at[3], f_r.at[2, 1], {Y: ym})
    far_out = wf.at[z, oxh, c]
    arrived(far_out, wo_r.at[0])
    weights_on(0, z, 1, 1)
    weights_on(1, z, 1, 1)
    weights_next(2, 0)
    send(far_out, far_out, wp_s.at[1], wp_r.at[3], partner)
    arrived(st_z.at[pl.ds(0, NZ - 1)], stat_r.at[3])
    st_all[c] = sum((st_z[k] for k in range(1, NZ)), st_z[0])
    send(st_all.at[c], st_all.at[c], stat_s.at[4], stat_r.at[4], partner)
    send(ft.at[me], ft.at[me], fp_s.at[0], fp_r.at[0], partner)
    load_a.wait()
    load_b.wait()
    arrived(st_all.at[oc], stat_r.at[4])
    store_stat = pltpu.make_async_copy(st_all, stat_hbm, out_sem.at[0])
    store_stat.start()

    inverse_rows = 1.0 / (ROWS * NZ * NX * NY * 2)

    def norm_grad(j):
        def one(i, carry):
            b = i * CHUNKS + j
            cols = pl.ds(pl.multiple_of(b * LANES, LANES), LANES)
            half, row = b // HALF, b % HALF
            plain = st_all[half, pl.ds(row, 1), :] * inverse_rows
            cross = st_all[half, pl.ds(HALF + row, 1), :] * inverse_rows
            scale = scale_b[pl.ds(b, 1), :] * scale_a[pl.ds(b, 1), :]
            value = msk[b].astype(F32) - plain - normed[:, cols].astype(F32) * cross
            ngs[b] = (scale * value).astype(BF16)
            return carry

        lax.fori_loop(0, NY * 2, one, 0)
        ngr[j, me] = ngs[me * CHUNKS + j]

    def block(chip, core, j):
        return ngs.at[(chip * 2 + core) * CHUNKS + j]

    def send_far(j):
        send(block(y2, 0, j), rel.at[0, j], ng_s.at[j], rel_r.at[0, j], {Y: yp})
        send(block(y2, 1, j), rel.at[1, j], ng_s.at[j], rel_r.at[1, j], {Y: ym})

    def send_near(j):
        for core in range(2):
            for chip in (yp, ym):
                send(block(chip, core, j), ngr.at[j, me], ng_s.at[j], near_r.at[j], {Y: chip, C: core})
        send(block(y, oc, j), ngr.at[j, me], ng_s.at[j], near_r.at[j], partner)

    def pass_on(j):
        arrived(rel.at[0, j], rel_r.at[0, j])
        send(rel.at[0, j], ngr.at[j, 2 * ym + c], ng_s.at[j], far_r.at[j], {Y: yp, C: 0})
        arrived(rel.at[1, j], rel_r.at[1, j])
        send(rel.at[1, j], ngr.at[j, 2 * yp + c], ng_s.at[j], far_r.at[j], {Y: ym, C: 1})

    tall = 256

    def product(j, rows, sources):
        a = jnp.concatenate([ft[s, rows, :] for s in sources], axis=1)
        b = jnp.concatenate([ngr[j, s] for s in sources], axis=0)
        return jnp.dot(a, b, preferred_element_type=F32)

    def multiply_near(j):
        arrived(ngr.at[j, pl.ds(0, 5)], near_r.at[j])

        def tile(i, carry):
            rows = pl.ds(pl.multiple_of(i * tall, tall), tall)
            near[rows, :] = product(j, rows, [2 * chip + core for chip in (y, yp, ym) for core in range(2)])
            return carry

        lax.fori_loop(0, DIN // tall, tile, 0)

    def multiply_far(j):
        arrived(ngr.at[j, pl.ds(0, 2)], far_r.at[j])

        def tile(i, carry):
            rows = pl.ds(pl.multiple_of(i * tall, tall), tall)
            out = (near[rows, :] + product(j, rows, [2 * y2, 2 * y2 + 1])).astype(STAGE_X)
            each = DIN // NZ
            share = each // NX
            for a in range(tall // each):
                for b in range(NX):
                    xs[j, b, i * (tall // each) + a] = out[a * each + b * share:a * each + (b + 1) * share]
            return carry

        lax.fori_loop(0, DIN // tall, tile, 0)
        for a, b in x_peers:
            send(xs.at[j, 2 * a + b], xr.at[j, x], x_s.at[j], x_r.at[j], {XH: a, XL: b})
        xr[j, x] = xs[j, x]

    def over_x(j):
        arrived(xr.at[j, pl.ds(0, NX - 1)], x_r.at[j])
        total = xr[j, 0].astype(F32)
        for k in range(1, NX):
            total += xr[j, k].astype(F32)
        zs[j] = total.astype(STAGE_Z)
        for k in (4, 3, 5, 2, 6, 1, 7):
            to = (z + k) % NZ
            send(zs.at[j, to], zr.at[j, z], z_s.at[j], z_r.at[j], {Z: to})
        zr[j, z] = zs[j, z]

    others = [(chip, lane) for chip in (y2, yp, ym) for lane in (oxl, xl)] + [(y, oxl)]

    def over_z(j):
        arrived(zr.at[j, pl.ds(0, NZ - 1)], z_r.at[j])
        total = zr[j, 0].astype(F32)
        for k in range(1, NZ):
            total += zr[j, k].astype(F32)
        gw[xl, y, c, j] = total
        mine = gw.at[xl, y, c, j]
        for chip, lane in others:
            send(mine, mine, g_s.at[j], g_r.at[j], {Y: chip, XL: lane})

    def gathered(j):
        arrived(near.at[pl.ds(0, len(others) * 32)], g_r.at[j])
        part = gw.at[:, :, c, j]
        send(part, part, gp_s.at[0], gp_r.at[j], partner)

    def grad_input(step):
        if step == 4:
            arrived(wf.at[pl.ds(0, 3), 0, 0], wp_r.at[3])
            blocks = (z, (z + 4) % NZ)
        else:
            arrived(wf.at[pl.ds(0, 2), :, 0], wp_r.at[step - 1])
            blocks = ((z - step + NZ) % NZ, (z + step) % NZ)
        acc[...] = jnp.zeros_like(acc)
        deep = 1024

        def part(i, carry):
            cols = pl.ds(pl.multiple_of(i * deep, deep), deep)
            count = deep // LANES
            a = jnp.concatenate([ngs[i * count + k] for k in range(count)], axis=1)
            b = jnp.concatenate([wf[k, :, :, :, cols].reshape(LANES, deep) for k in blocks], axis=0)
            acc[...] += lax.dot_general(a, b, (((1,), (1,)), ((), ())), preferred_element_type=F32)
            return carry

        lax.fori_loop(0, DOUT // deep, part, 0)
        for k, place in enumerate(blocks):
            cols = pl.ds(pl.multiple_of(place * LANES, LANES), LANES)
            gi[:, cols] = acc[:, k * LANES:(k + 1) * LANES].astype(BF16)

    def store(j):
        arrived(gw.at[:, :, oc, j], gp_r.at[j])
        copy = pltpu.make_async_copy(gw.at[:, :, :, j], gw_hbm.at[:, :, :, j], out_sem.at[2 + j])
        copy.start()
        return copy

    norm_grad(0)
    send_far(0)
    send_near(0)
    norm_grad(1)
    send_far(1)
    norm_grad(2)
    norm_grad(3)
    arrived(ft.at[2 * ym + c, pl.ds(0, mid)], f_r.at[1, 0])
    arrived(ft.at[2 * yp + c, pl.ds(0, mid)], f_r.at[1, 1])
    for chip in (ym, yp):
        send(ft.at[2 * chip + c], ft.at[2 * chip + c], fp_s.at[0], fp_r.at[0], partner)
    pass_on(0)
    send_far(2)
    send_near(1)
    for direction in range(2):
        arrived(ft.at[2 * y2 + c, pl.ds(direction * mid, mid)], f_r.at[2, direction])
    send(ft.at[2 * y2 + c], ft.at[2 * y2 + c], fp_s.at[0], fp_r.at[0], partner)
    pass_on(1)
    send_far(3)
    send_near(2)
    weights_next(1, 1)
    arrived(ft.at[pl.ds(0, 4)], fp_r.at[0])
    multiply_near(0)
    multiply_far(0)
    pass_on(2)
    send_near(3)
    weights_next(3, 0)
    multiply_near(1)
    multiply_far(1)
    pass_on(3)
    over_x(0)
    weights_next(2, 1)
    grad_input(1)
    multiply_near(2)
    multiply_far(2)
    over_x(1)
    weights_last(0)
    grad_input(2)
    multiply_near(3)
    multiply_far(3)
    over_z(0)
    over_x(2)
    over_z(1)
    weights_next(3, 1)
    grad_input(3)
    over_x(3)
    over_z(2)
    gathered(0)
    gathered(1)
    weights_last(1)
    grad_input(4)
    store_gi = pltpu.make_async_copy(gi, gi_hbm, out_sem.at[1])
    store_gi.start()
    over_z(3)
    gathered(2)
    stores = [store(j) for j in range(CHUNKS - 1)]
    gathered(3)
    stores.append(store(CHUNKS - 1))

    left(st.at[0], stat_s.at[0])
    left(st_y.at[pl.ds(0, NY - 1)], stat_s.at[1])
    left(st_x.at[pl.ds(0, NX - 1)], stat_s.at[2])
    left(st_z.at[pl.ds(0, NZ - 1)], stat_s.at[3])
    left(st.at[0], stat_s.at[4])
    for direction in range(2):
        left(ft.at[0], f_s.at[direction])
        left(low, f_s.at[2 + direction])
    left(ft.at[pl.ds(0, 4)], fp_s.at[0])
    left(far_out, wo_s.at[0])
    left(wf.at[pl.ds(0, 7), :, 0], wz_s.at[0])
    left(wf.at[pl.ds(0, 7), :, 0], wp_s.at[0])
    left(far_out, wp_s.at[1])
    for j in range(CHUNKS):
        left(ngs.at[pl.ds(0, 9)], ng_s.at[j])
        left(xr.at[j, pl.ds(0, NX - 1)], x_s.at[j])
        left(zr.at[j, pl.ds(0, NZ - 1)], z_s.at[j])
        left(near.at[pl.ds(0, len(others) * 32)], g_s.at[j])
    left(gw.at[:, :, c], gp_s.at[0])
    store_stat.wait()
    store_gi.wait()
    for copy in stores:
        copy.wait()


def finish(rescale, gi, gw, stat, gi_out, gw_out, gain, shift):
    gi_out[...] = gi[...]
    tall = gw.shape[2]
    for s in range(2):
        for b in range(BLOCKS):
            gw_out[s * tall:(s + 1) * tall, b * LANES:(b + 1) * LANES] = gw[s, b] * rescale
    for half in range(2):
        rows = slice(half * HALF, (half + 1) * HALF)
        shift[rows, :] = stat[half, :HALF] * rescale
        gain[rows, :] = stat[half, HALF:] * rescale


def on_device(features, normed, relu_mask, cotangent, weight_shard, norm_gain, inverse_deviation):
    dma = pltpu.SemaphoreType.DMA
    vmem = pltpu.VMEM
    any_space = pl.BlockSpec(memory_space=pl.ANY)
    rows_out = DIN // (NZ * NX)
    scratch = [
        vmem((ROWS, DIN), BF16), vmem((ROWS, DOUT), BF16), vmem((ROWS, DOUT), jnp.int32), vmem((ROWS, DOUT), BF16),
        vmem((BLOCKS, LANES), F32), vmem((BLOCKS, LANES), F32), vmem((BLOCKS, ROWS, LANES), BF16),
        vmem((NZ, 2, 2, 32, DOUT), BF16), vmem((NY * 2, DIN, ROWS), BF16),
        vmem((BLOCKS, ROWS, LANES), BF16), vmem((CHUNKS, NY * 2, ROWS, LANES), BF16), vmem((2, CHUNKS, ROWS, LANES), BF16),
        vmem((CHUNKS, NX, NZ, rows_out, LANES), STAGE_X), vmem((CHUNKS, NX, NZ, rows_out, LANES), STAGE_X),
        vmem((CHUNKS, NZ, rows_out, LANES), STAGE_Z), vmem((CHUNKS, NZ, rows_out, LANES), STAGE_Z),
        vmem((2, NY, 2, CHUNKS, rows_out, LANES), F32), vmem((ROWS, DIN), BF16), vmem((ROWS, 256), F32),
        vmem((DIN, LANES), F32),
        vmem((2, BLOCKS, LANES), F32), vmem((2, BLOCKS, LANES), F32), vmem((NX, BLOCKS, LANES), F32),
        vmem((NY, BLOCKS, LANES), F32), vmem((NZ, BLOCKS, LANES), F32), vmem((2, BLOCKS, LANES), F32),
        dma((4 + 3 * GROUPS,)), dma((2 + CHUNKS,)), dma((5,)), dma((5,)),
        dma((4,)), dma((3, 2)), dma((1,)), dma((1,)),
        dma((1,)), dma((1,)), dma((1,)), dma((2, 3, 2)), dma((2,)), dma((2,)), dma((4,)),
        dma((CHUNKS,)), dma((CHUNKS,)), dma((CHUNKS,)), dma((2, CHUNKS)),
        dma((CHUNKS,)), dma((CHUNKS,)), dma((CHUNKS,)), dma((CHUNKS,)), dma((CHUNKS,)), dma((CHUNKS,)), dma((1,)), dma((CHUNKS,)),
    ]
    grad_input, pieces, sums = pl.pallas_call(
        body,
        out_shape=(
            jax.ShapeDtypeStruct((ROWS, DIN), BF16),
            jax.ShapeDtypeStruct((2, NY, 2, CHUNKS, rows_out, LANES), F32),
            jax.ShapeDtypeStruct((2, BLOCKS, LANES), F32),
        ),
        in_specs=[any_space] * 7,
        out_specs=(any_space,) * 3,
        scratch_shapes=scratch,
        compiler_params=pltpu.CompilerParams(
            collective_id=0, has_side_effects=True, vmem_limit_bytes=56 * 1024 * 1024,
        ),
    )(
        features, normed, relu_mask, cotangent, weight_shard.reshape(2, 32, DOUT),
        norm_gain.reshape(BLOCKS, LANES), inverse_deviation.reshape(BLOCKS, LANES),
    )
    rescale = 1.0 / math.sqrt(ROWS * NZ * NX * NY * 2)
    grad_input, grad_weight, grad_gain, grad_shift = pl.pallas_call(
        functools.partial(finish, rescale),
        out_shape=(
            jax.ShapeDtypeStruct((ROWS, DIN), BF16),
            jax.ShapeDtypeStruct((2 * rows_out, DOUT), F32),
            jax.ShapeDtypeStruct((BLOCKS, LANES), F32),
            jax.ShapeDtypeStruct((BLOCKS, LANES), F32),
        ),
    )(grad_input, pieces.reshape(2, BLOCKS, rows_out, LANES), sums)
    return grad_input, grad_weight, grad_gain.reshape(DOUT), grad_shift.reshape(DOUT)


def solution(mesh):
    split = Mesh(mesh.devices.reshape(NZ, 2, NY, 2, 2), (Z, XH, Y, XL, C))
    rows = P((Z, XH, Y, XL, C), None)
    shard = P((Z, XH), None)
    return jax.shard_map(
        on_device,
        mesh=split,
        in_specs=(rows, rows, rows, rows, shard, P(), P()),
        out_specs=(rows, shard, P(), P()),
        check_vma=False,
    )
```

time: 88.4 us -> 77.6 us (0.88); the launches traced: 88.3 us -> 76.5 us
  Pallas kernels: 81.9 us -> 75.9 us
  local copies, waits for them, and re-layouts: 3.64 us -> 0 us
  other arithmetic: 2.09 us -> 0 us
    pallas_call x1, Pallas kernels: 81.9 us -> 73.3 us  [on_device(): pl.pallas_call(body, out_shape=(jax.ShapeDtypeStruct((ROWS, DIN), BF16),...]
    pallas_call x0 -> x1, Pallas kernels: none -> 2.57 us  [on_device(): pl.pallas_call(functools.partial(finish, rescale), out_shape=(jax.ShapeDt...]
    unnamed x4 -> x0, local copies, waits for them, and re-layouts: 2.37 us -> none
    mul x2 -> x0, other arithmetic: 2.09 us -> none  [the longest x1 1.32 us: on_device(): pieces.reshape(2, BLOCKS, rows_out, LANES).transpose(0, 2, 1, 3)]
where the time goes in v2:
time: 77.6 us; the launch traced here: 76.5 us
  Pallas kernels  75.9 us (98%)
    pallas_call x1, Pallas kernels, on_device(): pl.pallas_call(body, out_shape=(jax.ShapeDtypeStruct((ROWS, DIN), BF16),...  73.3 us
    pallas_call x1, Pallas kernels, on_device(): pl.pallas_call(functools.partial(finish, rescale), out_shape=(jax.ShapeDt...  2.57 us

profile of v2, /device:TPU:1, one launch (start us, length us, event | category | flops | bytes accessed | tf_op | source)
XLA Modules:
  0.0 76.5 jit_solution(12433245197241504579)
XLA Ops:
  0.6 73.3 %shard_map.102 = (bf16[256,1024]{1,0:T(8,128)(2,1)}, f32[2,4,2,4,32,128]{5,4,3,2,1,0:T(8,128)}, f32[2,32,128]{2,1,0:T(8,128)}) custom-call(bf16[256,1024]{1,0:T(8,128)(2,1)} %feat_hbm.1, bf16[256,4096]{1,0:T(8,128)(2,1)} %normed_hbm.1, s32[256,4096]{1,0:T(8,128)} %mask_hbm.1, bf16[256,4096]{1,0:T(8,128)(2,1)} %cot_hbm.1, bf16[2,32,4096]{2,1,0:T(8,128)(2,1)} %bitcast.7, ...), custom_call_target="tpu_custom_call" | custom-call | tf_op jit(solution)/shard_map/pallas_call | solution.py:443
  74.0 2.6 %shard_map.103 = (bf16[256,1024]{1,0:T(8,128)(2,1)}, f32[64,4096]{1,0:T(8,128)}, f32[32,128]{1,0:T(8,128)}, f32[32,128]{1,0:T(8,128)}) custom-call(bf16[256,1024]{1,0:T(8,128)(2,1)} %get-tuple-element.11.gi, f32[2,32,32,128]{3,2,1,0:T(8,128)} %bitcast.6, f32[2,32,128]{2,1,0:T(8,128)} %get-tuple-element.13.stat), custom_call_target="tpu_custom_call" | custom-call | tf_op jit(solution)/shard_map/pallas_call | solution.py:461

commit v3 on v2

--- a/solution.py
+++ b/solution.py
@@ -111,18 +111,28 @@
         ref = wf.at[block, side(o), c]
         send(ref, ref, wz_s.at[0], wz_r.at[direction, step - 1, o], {Z: zp if direction == 0 else zm})
 
-    def weights_next(step, o):
+    def weights_next(step, o, start=True):
         blocks = [(z + NZ - step) % NZ, (z + step) % NZ]
         for direction, b in enumerate(blocks):
-            arrived(wf.at[b, side(o), c], wz_r.at[direction, step - 1, o])
+            if start:
+                arrived(wf.at[b, side(o), c], wz_r.at[direction, step - 1, o])
             if step < 3:
                 weights_on(direction, b, step + 1, o)
         if step == 3:
-            ref = wf.at[(z + 5 - 2 * c) % NZ, side(o), c]
-            send(ref, ref, wz_s.at[0], wl_r.at[o], {Z: (z + 1 + 6 * c) % NZ})
+            for direction, b in enumerate(blocks):
+                ref = wf.at[b, side(o), c, pl.ds(direction * 16, 16)]
+                send(ref, ref, wz_s.at[0], wl_r.at[o], {Z: zp if direction == 0 else zm})
         for b in blocks:
             ref = wf.at[b, side(o), c]
             send(ref, ref, wp_s.at[0], wp_r.at[step - 1], partner)
+
+    def weights_over():
+        outer = {XH: oxh, XL: oxl}
+        for direction, b in enumerate(((z + NZ - 1) % NZ, (z + 1) % NZ)):
+            ref = wf.at[b, xh, c]
+            arrived(ref, wz_r.at[direction, 0, 0])
+            send(ref, ref, wo_s.at[0], wz_r.at[direction, 0, 1], outer)
+        send(wf.at[z, xh, c], wf.at[z, xh, c], wo_s.at[0], wo_r.at[0], outer)
 
     def weights_last(o):
         ref = wf.at[(z + 4) % NZ, side(o), c]
@@ -165,9 +175,7 @@
     st_x[x] = st_y[0] + st_y[1] + st_y[2] + st_y[3]
     for a, b in x_peers:
         send(st_x.at[x], st_x.at[x], stat_s.at[2], stat_r.at[2], {XH: a, XL: b})
-    outer = {XH: oxh, XL: oxl}
-    send(wf.at[z, xh, c], wf.at[z, xh, c], wo_s.at[0], wo_r.at[0], outer)
-    weights_next(1, 0)
+    weights_over()
     arrived(st_x.at[pl.ds(0, NX - 1)], stat_r.at[2])
     st_z[z] = st_x[0] + st_x[1] + st_x[2] + st_x[3]
     for k in (4, 3, 5, 2, 6, 1, 7):
@@ -178,12 +186,7 @@
     send(low, low, f_s.at[2], f_r.at[2, 0], {Y: yp})
     arrived(high, f_r.at[0, 1])
     send(high, high, f_s.at[3], f_r.at[2, 1], {Y: ym})
-    far_out = wf.at[z, oxh, c]
-    arrived(far_out, wo_r.at[0])
-    weights_on(0, z, 1, 1)
-    weights_on(1, z, 1, 1)
-    weights_next(2, 0)
-    send(far_out, far_out, wp_s.at[1], wp_r.at[3], partner)
+    weights_next(1, 0, start=False)
     arrived(st_z.at[pl.ds(0, NZ - 1)], stat_r.at[3])
     st_all[c] = sum((st_z[k] for k in range(1, NZ)), st_z[0])
     send(st_all.at[c], st_all.at[c], stat_s.at[4], stat_r.at[4], partner)
@@ -258,11 +261,12 @@
             for a in range(tall // each):
                 for b in range(NX):
                     xs[j, b, i * (tall // each) + a] = out[a * each + b * share:a * each + (b + 1) * share]
+            ready = pl.ds(i * (tall // each), tall // each)
+            for a, b in x_peers:
+                send(xs.at[j, 2 * a + b, ready], xr.at[j, x, ready], x_s.at[j], x_r.at[j], {XH: a, XL: b})
             return carry
 
         lax.fori_loop(0, DIN // tall, tile, 0)
-        for a, b in x_peers:
-            send(xs.at[j, 2 * a + b], xr.at[j, x], x_s.at[j], x_r.at[j], {XH: a, XL: b})
         xr[j, x] = xs[j, x]
 
     def over_x(j):
@@ -336,46 +340,50 @@
     pass_on(0)
     send_far(2)
     send_near(1)
+    weights_next(1, 1)
+    weights_next(2, 0)
     for direction in range(2):
         arrived(ft.at[2 * y2 + c, pl.ds(direction * mid, mid)], f_r.at[2, direction])
     send(ft.at[2 * y2 + c], ft.at[2 * y2 + c], fp_s.at[0], fp_r.at[0], partner)
     pass_on(1)
     send_far(3)
     send_near(2)
-    weights_next(1, 1)
+    far_out = wf.at[z, oxh, c]
+    arrived(far_out, wo_r.at[0])
+    send(far_out, far_out, wp_s.at[1], wp_r.at[3], partner)
     arrived(ft.at[pl.ds(0, 4)], fp_r.at[0])
     multiply_near(0)
     multiply_far(0)
     pass_on(2)
     send_near(3)
-    weights_next(3, 0)
     multiply_near(1)
+    weights_next(2, 1)
     multiply_far(1)
     pass_on(3)
     over_x(0)
-    weights_next(2, 1)
     grad_input(1)
+    weights_next(3, 0)
     multiply_near(2)
     multiply_far(2)
     over_x(1)
-    weights_last(0)
     grad_input(2)
+    weights_next(3, 1)
     multiply_near(3)
     multiply_far(3)
     over_z(0)
     over_x(2)
+    grad_input(3)
+    weights_last(0)
     over_z(1)
-    weights_next(3, 1)
-    grad_input(3)
     over_x(3)
+    weights_last(1)
     over_z(2)
     gathered(0)
-    gathered(1)
-    weights_last(1)
     grad_input(4)
     store_gi = pltpu.make_async_copy(gi, gi_hbm, out_sem.at[1])
     store_gi.start()
     over_z(3)
+    gathered(1)
     gathered(2)
     stores = [store(j) for j in range(CHUNKS - 1)]
     gathered(3)
@@ -390,8 +398,8 @@
         left(ft.at[0], f_s.at[direction])
         left(low, f_s.at[2 + direction])
     left(ft.at[pl.ds(0, 4)], fp_s.at[0])
-    left(far_out, wo_s.at[0])
-    left(wf.at[pl.ds(0, 7), :, 0], wz_s.at[0])
+    left(wf.at[pl.ds(0, 3), 0, 0], wo_s.at[0])
+    left(wf.at[pl.ds(0, 6), :, 0], wz_s.at[0])
     left(wf.at[pl.ds(0, 7), :, 0], wp_s.at[0])
     left(far_out, wp_s.at[1])
     for j in range(CHUNKS):
@@ -406,16 +414,44 @@
         copy.wait()
 
 
-def finish(rescale, gi, gw, stat, gi_out, gw_out, gain, shift):
-    gi_out[...] = gi[...]
+def finish(rescale, gi, gw, stat, gi_out, gw_out, gain_out, shift_out, gi_v, gw_v, stat_v, full, gain, shift, sems):
+    parts = gw_v.shape[0]
+    count = BLOCKS // (parts // 2)
     tall = gw.shape[2]
-    for s in range(2):
-        for b in range(BLOCKS):
-            gw_out[s * tall:(s + 1) * tall, b * LANES:(b + 1) * LANES] = gw[s, b] * rescale
+
+    def source(k):
+        return gw.at[k // 2, pl.ds(k % 2 * count, count)]
+
+    def target(k):
+        return gw_out.at[pl.ds(k // 2 * tall, tall), pl.ds(k % 2 * count * LANES, count * LANES)]
+
+    loads = [pltpu.make_async_copy(source(k), gw_v.at[k], sems.at[k]) for k in range(parts)]
+    loads.append(pltpu.make_async_copy(gi, gi_v, sems.at[parts]))
+    loads.append(pltpu.make_async_copy(stat, stat_v, sems.at[parts + 1]))
+    for copy in loads:
+        copy.start()
+    stores = []
+
+    def put(src, dst, sem):
+        stores.append(pltpu.make_async_copy(src, dst, sem))
+        stores[-1].start()
+
+    for k in range(parts):
+        loads[k].wait()
+        for b in range(count):
+            full[k, :, b * LANES:(b + 1) * LANES] = gw_v[k, b] * rescale
+        put(full.at[k], target(k), sems.at[parts + 2 + k])
+    loads[parts].wait()
+    put(gi_v, gi_out, sems.at[2 * parts + 2])
+    loads[parts + 1].wait()
     for half in range(2):
         rows = slice(half * HALF, (half + 1) * HALF)
-        shift[rows, :] = stat[half, :HALF] * rescale
-        gain[rows, :] = stat[half, HALF:] * rescale
+        shift[rows, :] = stat_v[half, :HALF] * rescale
+        gain[rows, :] = stat_v[half, HALF:] * rescale
+    put(gain, gain_out, sems.at[2 * parts + 3])
+    put(shift, shift_out, sems.at[2 * parts + 4])
+    for copy in stores:
+        copy.wait()
 
 
 def on_device(features, normed, relu_mask, cotangent, weight_shard, norm_gain, inverse_deviation):
@@ -457,6 +493,7 @@
         features, normed, relu_mask, cotangent, weight_shard.reshape(2, 32, DOUT),
         norm_gain.reshape(BLOCKS, LANES), inverse_deviation.reshape(BLOCKS, LANES),
     )
+    steps = 4
     rescale = 1.0 / math.sqrt(ROWS * NZ * NX * NY * 2)
     grad_input, grad_weight, grad_gain, grad_shift = pl.pallas_call(
         functools.partial(finish, rescale),
@@ -466,6 +503,13 @@
             jax.ShapeDtypeStruct((BLOCKS, LANES), F32),
             jax.ShapeDtypeStruct((BLOCKS, LANES), F32),
         ),
+        in_specs=[any_space] * 3,
+        out_specs=(any_space,) * 4,
+        scratch_shapes=[
+            vmem((ROWS, DIN), BF16), vmem((steps, 2 * BLOCKS // steps, rows_out, LANES), F32), vmem((2, BLOCKS, LANES), F32),
+            vmem((steps, rows_out, DOUT * 2 // steps), F32), vmem((BLOCKS, LANES), F32), vmem((BLOCKS, LANES), F32),
+            dma((2 * steps + 5,)),
+        ],
     )(grad_input, pieces.reshape(2, BLOCKS, rows_out, LANES), sums)
     return grad_input, grad_weight, grad_gain.reshape(DOUT), grad_shift.reshape(DOUT)
 

time: 77.6 us -> 74.1 us (0.955); the launches traced: 76.5 us -> 74 us
  Pallas kernels: 75.9 us -> 73.4 us
    pallas_call x1, Pallas kernels: 73.3 us -> 71.1 us  [on_device(): pl.pallas_call(body, out_shape=(jax.ShapeDtypeStruct((ROWS, DIN), BF16),...]
where the time goes in v3:
time: 74.1 us; the launch traced here: 74 us
  Pallas kernels  73.4 us (99%)
    pallas_call x1, Pallas kernels, on_device(): pl.pallas_call(body, out_shape=(jax.ShapeDtypeStruct((ROWS, DIN), BF16),...  71.1 us
    pallas_call x1, Pallas kernels, on_device(): pl.pallas_call(functools.partial(finish, rescale), out_shape=(jax.ShapeDt...  2.27 us

profile of v3, /device:TPU:1, one launch (start us, length us, event | category | flops | bytes accessed | tf_op | source)
XLA Modules:
  0.0 74.0 jit_solution(3702125179542306887)
XLA Ops:
  0.6 71.1 %shard_map.102 = (bf16[256,1024]{1,0:T(8,128)(2,1)}, f32[2,4,2,4,32,128]{5,4,3,2,1,0:T(8,128)}, f32[2,32,128]{2,1,0:T(8,128)}) custom-call(bf16[256,1024]{1,0:T(8,128)(2,1)} %feat_hbm.1, bf16[256,4096]{1,0:T(8,128)(2,1)} %normed_hbm.1, s32[256,4096]{1,0:T(8,128)} %mask_hbm.1, bf16[256,4096]{1,0:T(8,128)(2,1)} %cot_hbm.1, bf16[2,32,4096]{2,1,0:T(8,128)(2,1)} %bitcast.7, ...), custom_call_target="tpu_custom_call" | custom-call | tf_op jit(solution)/shard_map/pallas_call | solution.py:479
  71.7 2.3 %shard_map.103 = (bf16[256,1024]{1,0:T(8,128)(2,1)}, f32[64,4096]{1,0:T(8,128)}, f32[32,128]{1,0:T(8,128)}, f32[32,128]{1,0:T(8,128)}) custom-call(bf16[256,1024]{1,0:T(8,128)(2,1)} %get-tuple-element.11.gi, f32[2,32,32,128]{3,2,1,0:T(8,128)} %bitcast.6, f32[2,32,128]{2,1,0:T(8,128)} %get-tuple-element.13.stat), custom_call_target="tpu_custom_call" | custom-call | tf_op jit(solution)/shard_map/pallas_call | solution.py:498

commit v4 on v3

--- a/solution.py
+++ b/solution.py
@@ -221,15 +221,21 @@
         send(block(y2, 0, j), rel.at[0, j], ng_s.at[j], rel_r.at[0, j], {Y: yp})
         send(block(y2, 1, j), rel.at[1, j], ng_s.at[j], rel_r.at[1, j], {Y: ym})
 
-    def send_near(j):
-        for core in range(2):
+    def send_near_to(j, chip, core):
+        send(block(chip, core, j), ngr.at[j, me], ng_s.at[j], near_r.at[j], {Y: chip, C: core})
+
+    def send_near(j, cores=(0, 1)):
+        for core in cores:
             for chip in (yp, ym):
-                send(block(chip, core, j), ngr.at[j, me], ng_s.at[j], near_r.at[j], {Y: chip, C: core})
+                send_near_to(j, chip, core)
         send(block(y, oc, j), ngr.at[j, me], ng_s.at[j], near_r.at[j], partner)
 
-    def pass_on(j):
+    def pass_on(j, late=False):
         arrived(rel.at[0, j], rel_r.at[0, j])
         send(rel.at[0, j], ngr.at[j, 2 * ym + c], ng_s.at[j], far_r.at[j], {Y: yp, C: 0})
+        if late:
+            send_near_to(j, yp, 1)
+            send_near_to(j, ym, 1)
         arrived(rel.at[1, j], rel_r.at[1, j])
         send(rel.at[1, j], ngr.at[j, 2 * yp + c], ng_s.at[j], far_r.at[j], {Y: ym, C: 1})
 
@@ -354,35 +360,35 @@
     arrived(ft.at[pl.ds(0, 4)], fp_r.at[0])
     multiply_near(0)
     multiply_far(0)
+    send_near(3, (0,))
     pass_on(2)
-    send_near(3)
     multiply_near(1)
     weights_next(2, 1)
     multiply_far(1)
-    pass_on(3)
+    pass_on(3, late=True)
     over_x(0)
     grad_input(1)
     weights_next(3, 0)
     multiply_near(2)
     multiply_far(2)
     over_x(1)
-    grad_input(2)
-    weights_next(3, 1)
     multiply_near(3)
     multiply_far(3)
+    weights_next(3, 1)
     over_z(0)
     over_x(2)
-    grad_input(3)
+    grad_input(2)
     weights_last(0)
     over_z(1)
     over_x(3)
+    grad_input(3)
+    over_z(2)
     weights_last(1)
-    over_z(2)
     gathered(0)
+    over_z(3)
     grad_input(4)
     store_gi = pltpu.make_async_copy(gi, gi_hbm, out_sem.at[1])
     store_gi.start()
-    over_z(3)
     gathered(1)
     gathered(2)
     stores = [store(j) for j in range(CHUNKS - 1)]

time: 74.1 us -> 72.7 us (0.981)
  Pallas kernels: 73.4 us -> 72 us
    pallas_call x1, Pallas kernels: 71.1 us -> 69.7 us  [on_device(): pl.pallas_call(body, out_shape=(jax.ShapeDtypeStruct((ROWS, DIN), BF16),...]
where the time goes in v4:
time: 72.7 us; the launch traced here: 72.6 us
  Pallas kernels  72 us (99%)
    pallas_call x1, Pallas kernels, on_device(): pl.pallas_call(body, out_shape=(jax.ShapeDtypeStruct((ROWS, DIN), BF16),...  69.7 us
    pallas_call x1, Pallas kernels, on_device(): pl.pallas_call(functools.partial(finish, rescale), out_shape=(jax.ShapeDt...  2.27 us

profile of v4, /device:TPU:1, one launch (start us, length us, event | category | flops | bytes accessed | tf_op | source)
XLA Modules:
  0.0 72.6 jit_solution(950093794258827319)
XLA Ops:
  0.6 69.7 %shard_map.102 = (bf16[256,1024]{1,0:T(8,128)(2,1)}, f32[2,4,2,4,32,128]{5,4,3,2,1,0:T(8,128)}, f32[2,32,128]{2,1,0:T(8,128)}) custom-call(bf16[256,1024]{1,0:T(8,128)(2,1)} %feat_hbm.1, bf16[256,4096]{1,0:T(8,128)(2,1)} %normed_hbm.1, s32[256,4096]{1,0:T(8,128)} %mask_hbm.1, bf16[256,4096]{1,0:T(8,128)(2,1)} %cot_hbm.1, bf16[2,32,4096]{2,1,0:T(8,128)(2,1)} %bitcast.7, ...), custom_call_target="tpu_custom_call" | custom-call | tf_op jit(solution)/shard_map/pallas_call | solution.py:485
  70.3 2.3 %shard_map.103 = (bf16[256,1024]{1,0:T(8,128)(2,1)}, f32[64,4096]{1,0:T(8,128)}, f32[32,128]{1,0:T(8,128)}, f32[32,128]{1,0:T(8,128)}) custom-call(bf16[256,1024]{1,0:T(8,128)(2,1)} %get-tuple-element.11.gi, f32[2,32,32,128]{3,2,1,0:T(8,128)} %bitcast.6, f32[2,32,128]{2,1,0:T(8,128)} %get-tuple-element.13.stat), custom_call_target="tpu_custom_call" | custom-call | tf_op jit(solution)/shard_map/pallas_call | solution.py:504

commit v5 on v4

--- a/solution.py
+++ b/solution.py
@@ -372,9 +372,9 @@
     multiply_near(2)
     multiply_far(2)
     over_x(1)
+    weights_next(3, 1)
     multiply_near(3)
     multiply_far(3)
-    weights_next(3, 1)
     over_z(0)
     over_x(2)
     grad_input(2)
@@ -391,9 +391,9 @@
     store_gi.start()
     gathered(1)
     gathered(2)
-    stores = [store(j) for j in range(CHUNKS - 1)]
+    stores = [store(j) for j in range(CHUNKS - 2)]
     gathered(3)
-    stores.append(store(CHUNKS - 1))
+    stores += [store(j) for j in range(CHUNKS - 2, CHUNKS)]
 
     left(st.at[0], stat_s.at[0])
     left(st_y.at[pl.ds(0, NY - 1)], stat_s.at[1])

time: 72.7 us -> 74.1 us (1.019)
  Pallas kernels: 72 us -> 73.4 us
    pallas_call x1, Pallas kernels: 69.7 us -> 71.1 us  [on_device(): pl.pallas_call(body, out_shape=(jax.ShapeDtypeStruct((ROWS, DIN), BF16),...]
where the time goes in v5:
time: 74.1 us; the launch traced here: 74 us
  Pallas kernels  73.4 us (99%)
    pallas_call x1, Pallas kernels, on_device(): pl.pallas_call(body, out_shape=(jax.ShapeDtypeStruct((ROWS, DIN), BF16),...  71.1 us
    pallas_call x1, Pallas kernels, on_device(): pl.pallas_call(functools.partial(finish, rescale), out_shape=(jax.ShapeDt...  2.27 us

profile of v5, /device:TPU:1, one launch (start us, length us, event | category | flops | bytes accessed | tf_op | source)
XLA Modules:
  0.0 74.0 jit_solution(8613442538047748050)
XLA Ops:
  0.6 71.1 %shard_map.102 = (bf16[256,1024]{1,0:T(8,128)(2,1)}, f32[2,4,2,4,32,128]{5,4,3,2,1,0:T(8,128)}, f32[2,32,128]{2,1,0:T(8,128)}) custom-call(bf16[256,1024]{1,0:T(8,128)(2,1)} %feat_hbm.1, bf16[256,4096]{1,0:T(8,128)(2,1)} %normed_hbm.1, s32[256,4096]{1,0:T(8,128)} %mask_hbm.1, bf16[256,4096]{1,0:T(8,128)(2,1)} %cot_hbm.1, bf16[2,32,4096]{2,1,0:T(8,128)(2,1)} %bitcast.7, ...), custom_call_target="tpu_custom_call" | custom-call | tf_op jit(solution)/shard_map/pallas_call | solution.py:485
  71.7 2.3 %shard_map.103 = (bf16[256,1024]{1,0:T(8,128)(2,1)}, f32[64,4096]{1,0:T(8,128)}, f32[32,128]{1,0:T(8,128)}, f32[32,128]{1,0:T(8,128)}) custom-call(bf16[256,1024]{1,0:T(8,128)(2,1)} %get-tuple-element.11.gi, f32[2,32,32,128]{3,2,1,0:T(8,128)} %bitcast.6, f32[2,32,128]{2,1,0:T(8,128)} %get-tuple-element.13.stat), custom_call_target="tpu_custom_call" | custom-call | tf_op jit(solution)/shard_map/pallas_call | solution.py:504

commit v6 on v5

--- a/solution.py
+++ b/solution.py
@@ -372,9 +372,9 @@
     multiply_near(2)
     multiply_far(2)
     over_x(1)
-    weights_next(3, 1)
     multiply_near(3)
     multiply_far(3)
+    weights_next(3, 1)
     over_z(0)
     over_x(2)
     grad_input(2)

time: 74.1 us -> 72.7 us (0.981)
  Pallas kernels: 73.4 us -> 72 us
    pallas_call x1, Pallas kernels: 71.1 us -> 69.7 us  [on_device(): pl.pallas_call(body, out_shape=(jax.ShapeDtypeStruct((ROWS, DIN), BF16),...]
where the time goes in v6:
time: 72.7 us; the launch traced here: 72.6 us
  Pallas kernels  72 us (99%)
    pallas_call x1, Pallas kernels, on_device(): pl.pallas_call(body, out_shape=(jax.ShapeDtypeStruct((ROWS, DIN), BF16),...  69.7 us
    pallas_call x1, Pallas kernels, on_device(): pl.pallas_call(functools.partial(finish, rescale), out_shape=(jax.ShapeDt...  2.27 us

profile of v6, /device:TPU:1, one launch (start us, length us, event | category | flops | bytes accessed | tf_op | source)
XLA Modules:
  0.0 72.6 jit_solution(10114174301786695277)
XLA Ops:
  0.6 69.7 %shard_map.102 = (bf16[256,1024]{1,0:T(8,128)(2,1)}, f32[2,4,2,4,32,128]{5,4,3,2,1,0:T(8,128)}, f32[2,32,128]{2,1,0:T(8,128)}) custom-call(bf16[256,1024]{1,0:T(8,128)(2,1)} %feat_hbm.1, bf16[256,4096]{1,0:T(8,128)(2,1)} %normed_hbm.1, s32[256,4096]{1,0:T(8,128)} %mask_hbm.1, bf16[256,4096]{1,0:T(8,128)(2,1)} %cot_hbm.1, bf16[2,32,4096]{2,1,0:T(8,128)(2,1)} %bitcast.7, ...), custom_call_target="tpu_custom_call" | custom-call | tf_op jit(solution)/shard_map/pallas_call | solution.py:485
  70.3 2.3 %shard_map.103 = (bf16[256,1024]{1,0:T(8,128)(2,1)}, f32[64,4096]{1,0:T(8,128)}, f32[32,128]{1,0:T(8,128)}, f32[32,128]{1,0:T(8,128)}) custom-call(bf16[256,1024]{1,0:T(8,128)(2,1)} %get-tuple-element.11.gi, f32[2,32,32,128]{3,2,1,0:T(8,128)} %bitcast.6, f32[2,32,128]{2,1,0:T(8,128)} %get-tuple-element.13.stat), custom_call_target="tpu_custom_call" | custom-call | tf_op jit(solution)/shard_map/pallas_call | solution.py:504
